TPU v7x, 32 devices: a whole 2x2x4 slice. The times are simulated.
32 devices in a mesh: heads: 4 (over y, x), seq: 8 (over z, core).
Axes of the slice: x: 2, y: 2, z: 4, core: 2. Of those that a mesh axis runs over, the one named last changes fastest.
Arguments:
- local_qkv: bfloat16 [3, 4096, 2048], P(None, 'seq', 'heads'), may hold values from -8 to 8
- routed_qkv: bfloat16 [3, 4096, 2048], P(None, 'seq', 'heads'), may hold values from -8 to 8
- clusters: int32 [16, 4096], P('heads', 'seq'), may hold values from 0 to 127, as said below
- wo_local: bfloat16 [2048, 4096], P('heads'), may hold values from -0.5 to 0.5
- wo_routed: bfloat16 [2048, 4096], P('heads'), may hold values from -0.5 to 0.5
Outputs:
- layer_out: bfloat16 [4096, 4096], P('seq', 'heads')
Inputs may be any that keep to these rules, and one draw needn't show every extreme that they name: `clusters`: in every routed head, no cluster holds more than 8 of the 512 tokens of one aligned block of tokens; in every head and block some cluster holds exactly 8 of them.
All inputs are finite; a program needn't handle non-finite values.
Results may differ from a plain program's by a relative error of at most 0.009.
Values may be sent and summed in bfloat16 or wider, within the bound.
A program may use at most 128 MiB of HBM per device.

v0:
```python
import jax
import jax.numpy as jnp
from jax import lax
from jax.sharding import PartitionSpec as P

DH = 128
WINDOW = 512
NCLUST = 128
masked_fill = -1e30


def passed_along(block, axis, distance):
    devices = range(lax.axis_size(axis))
    route = [(i - distance, i) for i in devices if i - distance in devices]
    return lax.ppermute(block, axis, route)


def soft_weights(scores, allowed):
    scores = jnp.where(allowed, scores, masked_fill)
    top_score = jnp.max(scores, axis=-1, keepdims=True)
    raised = jnp.exp(scores - top_score)
    return (raised / jnp.sum(raised, axis=-1, keepdims=True)).astype(jnp.bfloat16)


def window_part(local_qkv):
    tok_count = local_qkv.shape[1]
    width = local_qkv.shape[2]
    head_count = width // DH
    seq_index = lax.axis_index("seq")
    earlier = passed_along(local_qkv[1:], "seq", 1)
    joined = jnp.concatenate([earlier, local_qkv[1:]], axis=1)
    queries = local_qkv[0].reshape(tok_count, head_count, DH)
    keys_all = joined[0].reshape(2 * tok_count, head_count, DH)
    values_all = joined[1].reshape(2 * tok_count, head_count, DH)

    def one_block(index):
        start = index * WINDOW
        scores = jnp.einsum(
            "qhd,khd->hqk", queries, keys_all, preferred_element_type=jnp.float32
        ) * DH ** (-0.5)
        query_at = start + jnp.arange(WINDOW, dtype=jnp.int32)
        key_index = tok_count + start - WINDOW + jnp.arange(2 * WINDOW, dtype=jnp.int32)
        offset = (key_index - tok_count)[None, :] - query_at[:, None]
        present = (seq_index > 0) | (key_index >= tok_count)
        allowed = (offset <= 0) & (offset > -WINDOW) & present[None, :]
        weights = soft_weights(scores, allowed[None])
        result = jnp.einsum("hqk,khd->qhd", weights, values_all, preferred_element_type=jnp.float32)
        return result.astype(jnp.bfloat16).reshape(WINDOW, width)

    blocks = lax.map(one_block, jnp.arange(tok_count // WINDOW, dtype=jnp.int32))
    return blocks.reshape(tok_count, width)


def routed_part(routed_qkv, clusters):
    tok_count = routed_qkv.shape[1]
    head_count = clusters.shape[0]
    seq_count = lax.axis_size("seq")
    seq_index = lax.axis_index("seq")
    most_rows = 2 * tok_count // NCLUST
    slot_total = NCLUST * most_rows
    per_owner = slot_total // seq_count
    onehot = (clusters[:, :, None] == jnp.arange(NCLUST, dtype=jnp.int32)[None, None, :]).astype(
        jnp.int32
    )
    before = jnp.cumsum(onehot, axis=1) - onehot
    rank_index = jnp.sum(before * onehot, axis=-1)
    slot_index = clusters * most_rows + rank_index
    head_index = jnp.broadcast_to(
        jnp.arange(head_count, dtype=jnp.int32)[:, None], (head_count, tok_count)
    )
    token_ids = jnp.broadcast_to(
        jnp.arange(tok_count, dtype=jnp.int32)[None, :], (head_count, tok_count)
    )
    token_at = (
        jnp.full((head_count, slot_total), -1, jnp.int32).at[head_index, slot_index].set(token_ids)
    )
    row_data = (
        routed_qkv.reshape(3, tok_count, head_count, DH)
        .transpose(2, 1, 0, 3)
        .reshape(head_count, tok_count, 3 * DH)
    )
    picked = jnp.take_along_axis(row_data, jnp.maximum(token_at, 0)[:, :, None], axis=1)
    picked = jnp.where(token_at[:, :, None] >= 0, picked, jnp.zeros_like(picked))
    positions = jnp.where(token_at >= 0, seq_index * tok_count + token_at, -1)
    send_rows = picked.reshape(head_count, seq_count, per_owner, 3 * DH)
    send_places = positions.reshape(head_count, seq_count, per_owner)
    rows_in = lax.all_to_all(send_rows, "seq", split_axis=1, concat_axis=1, tiled=True)
    places_in = lax.all_to_all(send_places, "seq", split_axis=1, concat_axis=1, tiled=True)
    item_count = rows_in.shape[0]
    owned = per_owner // most_rows
    members = seq_count * most_rows
    grouped = rows_in.reshape(item_count, seq_count, owned, most_rows, 3 * DH).transpose(
        0, 2, 1, 3, 4
    )
    grouped = grouped.reshape(item_count, owned, members, 3 * DH)
    places = places_in.reshape(item_count, seq_count, owned, most_rows).transpose(0, 2, 1, 3)
    places = places.reshape(item_count, owned, members)
    scores = jnp.einsum(
        "ncqd,nckd->ncqk",
        grouped[..., :DH],
        grouped[..., DH : 2 * DH],
        preferred_element_type=jnp.float32,
    ) * DH ** (-0.5)
    allowed = (places[:, :, None, :] >= 0) & (places[:, :, None, :] <= places[:, :, :, None])
    weights = soft_weights(scores, allowed)
    result = jnp.einsum(
        "ncqk,nckd->ncqd", weights, grouped[..., 2 * DH :], preferred_element_type=jnp.float32
    )
    result = (
        result.astype(jnp.bfloat16)
        .reshape(item_count, owned, seq_count, most_rows, DH)
        .transpose(0, 2, 1, 3, 4)
    )
    result = result.reshape(item_count, seq_count, per_owner, DH)
    returned = lax.all_to_all(result, "seq", split_axis=1, concat_axis=1, tiled=True)
    returned = returned.reshape(head_count, slot_total, DH)
    mine = jnp.take_along_axis(returned, slot_index[:, :, None], axis=1)
    return mine.transpose(1, 0, 2).reshape(tok_count, head_count * DH)


def body(local_qkv, routed_qkv, clusters, wo_local, wo_routed):
    local_out = window_part(local_qkv)
    routed_out = routed_part(routed_qkv, clusters)
    group_sum = jnp.dot(local_out, wo_local, preferred_element_type=jnp.float32)
    group_sum = group_sum + jnp.dot(routed_out, wo_routed, preferred_element_type=jnp.float32)
    summed = lax.psum_scatter(
        group_sum.astype(jnp.bfloat16), "heads", scatter_dimension=1, tiled=True
    )
    return summed


def solution(mesh):
    return jax.shard_map(
        body,
        mesh=mesh,
        in_specs=(
            P(None, "seq", "heads"),
            P(None, "seq", "heads"),
            P("heads", "seq"),
            P("heads", None),
            P("heads", None),
        ),
        out_specs=P("seq", "heads"),
        check_vma=False,
    )
```

profile of v0, /device:TPU:0, one launch (start us, length us, event | category | flops | bytes accessed | tf_op | source)
XLA Modules:
  0.0 282.5 jit_solution(4169439975950401828)
XLA Ops:
  6.5 0.7 eq.26
  7.4 0.9 fusion.21
  9.0 0.6 fusion.19
  9.9 8.1 %scatter_custom_fusion = s32[4096]{0:T(1024)S(1)} fusion(s32[2048]{0:T(1024)S(1)} %bitcast.109, s32[2048]{0:T(1024)S(1)} %bitcast.108, s32[]{:T(128)} %constant.87.clone.1), kind=kCustom, calls=%fused_computation.62 | custom fusion | bytes 16388
  18.0 0.6 copy.75
  18.6 6.3 %all-to-all-start = ((s32[4,8,128]{2,0,1:T(4,128)}), s32[4,8,128]{2,0,1:T(4,128)S(1)}, u32[]{:S(2)}, u32[]{:S(2)}) async-start(s32[4,8,128]{2,0,1:T(4,128)} %copy.75), calls=%async_computation | async-start | bytes 32768 | tf_op jit(solution)/shard_map/all_to_all | solution.py:88
  25.0 0.7 copy.83
  25.8 0.9 copy.85
  26.7 44.7 %gather_fusion = bf16[4096,384]{1,0:T(8,128)(2,1)} fusion(bf16[4,512,384]{2,1,0:T(8,128)(2,1)S(1)} %copy.85, s32[4096]{0:T(1024)S(1)} %bitcast.93), kind=kCustom, calls=%fused_computation | custom fusion | bytes 6324224 | tf_op jit(solution)/shard_map/jit(take_along_axis)/gather | solution.py:82
  71.5 4.8 %fusion.7 = bf16[4,8,128,384]{3,2,0,1:T(8,128)(2,1)} fusion(bf16[4,8,128,384]{3,2,1,0:T(8,128)(2,1)} %bitcast.96, pred[4,8,128]{2,0,1:T(4,128)(4,1)S(1)} %copy.82, pred[4,8,128]{2,0,1:T(4,128)(4,1)S(1)} %copy.81), kind=kLoop, calls=%fused_computation.16 | loop fusion | flops 3145728 | bytes 6299648 | tf_op jit(solution)/shard_map/jit(_where)/select_n | solution.py:83
  76.3 5.1 %all-to-all-start.1 = ((bf16[4,8,128,384]{3,2,0,1:T(8,128)(2,1)}), bf16[4,8,128,384]{3,2,0,1:T(8,128)(2,1)S(1)}, u32[]{:S(2)}, u32[]{:S(2)}) async-start(bf16[4,8,128,384]{3,2,0,1:T(8,128)(2,1)} %fusion.7), calls=%async_computation.1 | async-start | bytes 6291456 | tf_op jit(solution)/shard_map/all_to_all | solution.py:87
  81.4 2.3 slice.28
  83.6 2.3 copy.99
  85.9 3.4 %collective-permute-start = (bf16[2,512,512]{1,2,0:T(8,128)(2,1)}, bf16[2,512,512]{1,2,0:T(8,128)(2,1)}, u32[]{:S(2)}, u32[]{:S(2)}) collective-permute-start(bf16[2,512,512]{1,2,0:T(8,128)(2,1)} %copy.99), channel_id=1, source_target_pairs={{0,1},{1,2},{2,3},{3,4},{4,5},{5,6},{6,7},{8,9},{9,10},{10,11},{11... | collective-permute-start | bytes 3145736 | tf_op jit(solution)/shard_map/ppermute | solution.py:15
  89.3 1.9 slice.31
  91.2 2.1 copy.100
  93.3 1.6 fusion.11
  95.4 3.2 %pad_maximum_fusion = (bf16[1,1024,512]{1,2,0:T(8,128)(2,1)}, bf16[1,1024,512]{1,2,0:T(8,128)(2,1)}) fusion(bf16[2,512,512]{1,2,0:T(8,128)(2,1)} %copy.99, bf16[2,512,512]{1,2,0:T(8,128)(2,1)} %collective-permute-done), kind=kLoop, calls=%fused_computation.34 | loop fusion | flops 4194304 | bytes 4194304 | tf_op jit(solution)/shard_map/concatenate | solution.py:31
  98.6 54.3 %all-to-all-done.1 = bf16[4,8,128,384]{3,2,0,1:T(8,128)(2,1)S(1)} async-done(((bf16[4,8,128,384]{3,2,0,1:T(8,128)(2,1)}), bf16[4,8,128,384]{3,2,0,1:T(8,128)(2,1)S(1)}, u32[]{:S(2)}, u32[]{:S(2)}) %all-to-all-start.1) | async-done | bytes 3145760 | tf_op jit(solution)/shard_map/all_to_all | solution.py:87
  152.9 0.6 copy_bitcast_fusion
  153.5 3.2 %multiply_select_fusion = f32[4,16,64,64]{2,3,1,0:T(8,128)S(1)} fusion(bf16[4,16,64,384]{3,2,1,0:T(8,128)(2,1)S(1)} %copy_bitcast_fusion, s32[4,16,64]{2,1,0:T(8,128)S(1)} %copy.79, pred[4,16,64]{2,1,0:T(8,128)(4,1)S(1)} %copy.78), kind=kOutput, calls=%fused_computation.21 | convolution fusion | flops 68157440 | bytes 3219456 | tf_op jit(solution)/shard_map/ncqd,nckd->ncqk/dot_general | solution.py:98
  156.7 0.5 fusion.35
  157.2 2.0 fusion.12
  159.5 1.0 copy.91
  160.6 16.2 %all-to-all-start.2 = ((bf16[4,8,128,128]{3,2,0,1:T(8,128)(2,1)}), bf16[4,8,128,128]{3,2,0,1:T(8,128)(2,1)S(1)}, u32[]{:S(2)}, u32[]{:S(2)}) async-start(bf16[4,8,128,128]{3,2,0,1:T(8,128)(2,1)} %copy.91), calls=%async_computation.2 | async-start | bytes 2097152 | tf_op jit(solution)/shard_map/all_to_all | solution.py:115
  177.0 7.9 %fusion.34 = (f32[4,512]{1,0:T(4,128)S(1)}, f32[4,512,1024]{1,2,0:T(8,128)}) fusion(pred[512,1024]{0,1:T(8,128)(4,1)} %fusion.11, bf16[1024,4,128]{0,2,1:T(8,128)(2,1)S(1)} %bitcast.105, bf16[512,4,128]{0,2,1:T(8,128)(2,1)} %bitcast.107), kind=kOutput, calls=%fused_computation.74 | convolution fusion | flops 545260544 | bytes 10493952 | tf_op jit(solution)/shard_map/while/body/eval_jaxpr/sub | solution.py:21
  184.9 4.3 %fusion.13 = bf16[4,128,512]{2,1,0:T(8,128)(2,1)S(1)} fusion(bf16[1024,4,128]{0,2,1:T(8,128)(2,1)S(1)} %bitcast.104, f32[4,512,1024]{1,2,0:T(8,128)} %get-tuple-element.30, f32[4,512]{1,0:T(4,128)S(1)} %get-tuple-element.29), kind=kOutput, calls=%fused_computation.29 | convolution fusion | flops 541327360 | bytes 9969664 | tf_op jit(solution)/shard_map/while/body/eval_jaxpr/hqk,khd->qhd/dot_general | solution.py:47
  189.5 5.6 %fusion.36 = f32[512,4096]{1,0:T(8,128)} fusion(bf16[512,512]{0,1:T(8,128)(2,1)S(1)} %bitcast.106, bf16[512,4096]{1,0:T(8,128)(2,1)S(1)} %copy-done), kind=kOutput, calls=%fused_computation.76 | convolution fusion | flops 2147483648 | bytes 13107200 | tf_op jit(solution)/shard_map/dot_general | solution.py:124
  195.0 8.3 %all-to-all-done.2 = bf16[4,8,128,128]{3,2,0,1:T(8,128)(2,1)S(1)} async-done(((bf16[4,8,128,128]{3,2,0,1:T(8,128)(2,1)}), bf16[4,8,128,128]{3,2,0,1:T(8,128)(2,1)S(1)}, u32[]{:S(2)}, u32[]{:S(2)}) %all-to-all-start.2) | async-done | bytes 1048608 | tf_op jit(solution)/shard_map/all_to_all | solution.py:115
  203.4 11.1 %gather_fusion.1 = bf16[2048,128]{1,0:T(8,128)(2,1)S(1)} fusion(bf16[4,1024,128]{2,1,0:T(8,128)(2,1)S(1)} %bitcast.95, s32[2048]{0:T(1024)S(1)} %bitcast.94), kind=kCustom, calls=%fused_computation.1 | custom fusion | bytes 1064960 | tf_op jit(solution)/shard_map/jit(take_along_axis)/gather | solution.py:117
  214.9 9.0 %add_convert_fusion = bf16[512,4096]{1,0:T(8,128)(2,1)} fusion(f32[512,4096]{1,0:T(8,128)} %fusion.36, bf16[512,512]{0,1:T(8,128)(2,1)S(1)} %bitcast.100, bf16[512,4096]{1,0:T(8,128)(2,1)} %param.9), kind=kOutput, calls=%fused_computation.6 | convolution fusion | flops 2151677952 | bytes 17301504 | tf_op jit(solution)/shard_map/dot_general | solution.py:125
  223.9 51.7 %reduce-scatter.2.cloned.1.call-done = bf16[512,1024]{1,0:T(8,128)(2,1)} async-done(((bf16[512,4096]{1,0:T(8,128)(2,1)}), bf16[512,1024]{1,0:T(8,128)(2,1)}) %reduce-scatter.2.cloned.1.call-update) | async-done | bytes 1048592 | tf_op jit(solution)/shard_map/reduce_scatter | solution.py:126
  (57 shorter events, 2.9 us)
Async XLA Ops:
  8.3 0.7 copy-start.5
  8.5 1.2 copy-start.7
  8.5 1.2 copy-start.6
  8.6 16.5 %copy-start.2 = (bf16[3,512,512]{2,1,0:T(8,128)(2,1)S(1)}, bf16[3,512,512]{2,1,0:T(8,128)(2,1)}, u32[]{:S(2)}) copy-start(bf16[3,512,512]{2,1,0:T(8,128)(2,1)} %param.6) | copy-start | bytes 4718596
  18.6 57.7 %all-to-all-start = ((s32[4,8,128]{2,0,1:T(4,128)}), s32[4,8,128]{2,0,1:T(4,128)S(1)}, u32[]{:S(2)}, u32[]{:S(2)}) async-start(s32[4,8,128]{2,0,1:T(4,128)} %copy.75), calls=%async_computation | async-start | bytes 32768 | tf_op jit(solution)/shard_map/all_to_all | solution.py:88
  76.3 76.6 %all-to-all-start.1 = ((bf16[4,8,128,384]{3,2,0,1:T(8,128)(2,1)}), bf16[4,8,128,384]{3,2,0,1:T(8,128)(2,1)S(1)}, u32[]{:S(2)}, u32[]{:S(2)}) async-start(bf16[4,8,128,384]{3,2,0,1:T(8,128)(2,1)} %fusion.7), calls=%async_computation.1 | async-start | bytes 6291456 | tf_op jit(solution)/shard_map/all_to_all | solution.py:87
  85.9 9.5 %collective-permute-start = (bf16[2,512,512]{1,2,0:T(8,128)(2,1)}, bf16[2,512,512]{1,2,0:T(8,128)(2,1)}, u32[]{:S(2)}, u32[]{:S(2)}) collective-permute-start(bf16[2,512,512]{1,2,0:T(8,128)(2,1)} %copy.99), channel_id=1, source_target_pairs={{0,1},{1,2},{2,3},{3,4},{4,5},{5,6},{6,7},{8,9},{9,10},{10,11},{11... | collective-permute-start | bytes 3145736 | tf_op jit(solution)/shard_map/ppermute | solution.py:15
  153.5 3.2 %copy-start.1 = (bf16[4,16,64,384]{3,2,1,0:T(8,128)(2,1)}, bf16[4,16,64,384]{3,2,1,0:T(8,128)(2,1)S(1)}, u32[]{:S(2)}) copy-start(bf16[4,16,64,384]{3,2,1,0:T(8,128)(2,1)S(1)} %copy_bitcast_fusion) | copy-start | bytes 9437188
  159.5 17.5 %copy-start.4 = (bf16[1,1024,512]{1,2,0:T(8,128)(2,1)S(1)}, bf16[1,1024,512]{1,2,0:T(8,128)(2,1)}, u32[]{:S(2)}) copy-start(bf16[1,1024,512]{1,2,0:T(8,128)(2,1)} %get-tuple-element.15) | copy-start | bytes 3145732
  160.6 42.8 %all-to-all-start.2 = ((bf16[4,8,128,128]{3,2,0,1:T(8,128)(2,1)}), bf16[4,8,128,128]{3,2,0,1:T(8,128)(2,1)S(1)}, u32[]{:S(2)}, u32[]{:S(2)}) async-start(bf16[4,8,128,128]{3,2,0,1:T(8,128)(2,1)} %copy.91), calls=%async_computation.2 | async-start | bytes 2097152 | tf_op jit(solution)/shard_map/all_to_all | solution.py:115
  176.7 98.9 %reduce-scatter.2.cloned.1.call-start = ((), (), s32[]{:S(2)}) async-start(), calls=%async_computation.4 | async-start | bytes 5242880 | tf_op jit(solution)/shard_map/reduce_scatter | solution.py:126
  177.0 7.9 %copy-start.3 = (bf16[1,1024,512]{1,2,0:T(8,128)(2,1)S(1)}, bf16[1,1024,512]{1,2,0:T(8,128)(2,1)}, u32[]{:S(2)}) copy-start(bf16[1,1024,512]{1,2,0:T(8,128)(2,1)} %get-tuple-element.16) | copy-start | bytes 3145732
  184.9 4.6 %copy-start = (bf16[512,4096]{1,0:T(8,128)(2,1)S(1)}, bf16[512,4096]{1,0:T(8,128)(2,1)}, u32[]{:S(2)}) copy-start(bf16[512,4096]{1,0:T(8,128)(2,1)} %param.8) | copy-start | bytes 12582916
Sparse Core Ops, SparseCore 0:
  224.0 51.5 reduce-scatter.1
where the time goes:
time: 283 us
  waiting for transfers between devices  114 us (40%)
  local copies, waits for them, and re-layouts  79 us (28%)
  matrix products  32 us (11%)
  starting transfers between devices  31.2 us (11%)
  between operations  13.8 us (5%)
  other arithmetic  12.2 us (4%)
    all_to_all x1, waiting for transfers between devices, routed_part(): lax.all_to_all(send_rows, 'seq', split_axis=1, concat_axis=1, tiled=True)  54.3 us
    reduce_scatter x1, waiting for transfers between devices, body(): lax.psum_scatter(group_sum.astype(jnp.bfloat16), 'heads', scatter_dimensi...  51.7 us
    gather x2, local copies, waits for them, and re-layouts, routed_part(): jnp.take_along_axis(row_data, jnp.maximum(token_at, 0)[:, :, None], axis=1)  44.8 us
    all_to_all x1, starting transfers between devices, routed_part(): lax.all_to_all(result, 'seq', split_axis=1, concat_axis=1, tiled=True)  16.2 us
    unnamed x25, local copies, waits for them, and re-layouts  13.7 us
    gather x2, local copies, waits for them, and re-layouts, routed_part(): mine = jnp.take_along_axis(returned, slot_index[:, :, None], axis=1)  11.3 us
    dot_general x1, matrix products, body(): jnp.dot(routed_out, wo_routed, preferred_element_type=jnp.float32)  9.04 us
    all_to_all x1, waiting for transfers between devices, routed_part(): lax.all_to_all(result, 'seq', split_axis=1, concat_axis=1, tiled=True)  8.28 us
  transfers between devices with their start and end apart: 5, of which 3 were waited for; matrix products, arithmetic and copies ran while one was open for 29% of the time, Pallas kernels for 0%

commit v1 on v0

--- a/solution.py
+++ b/solution.py
@@ -7,6 +7,27 @@
 WINDOW = 512
 NCLUST = 128
 masked_fill = -1e30
+
+
+def order_sums_all(z):
+    axis_tag = "seq"
+    clean = lax.axis_size(axis_tag)
+    near = lax.axis_index(axis_tag)
+    val, state_next = (clean, near)
+    reached = z.shape[1] // val
+    view_out = list(z.shape)
+    view_out[1] = reached
+    oldest = view_out[1]
+    view_out[1] = oldest * val
+    seen_now = jnp.zeros(view_out, z.dtype)
+    for j0 in range(val):
+        s_next = lax.dynamic_slice_in_dim(z, (state_next ^ j0) * reached, reached, axis=1)
+        if j0:
+            s_next = lax.ppermute(s_next, axis_tag, perm=[(num, num ^ j0) for num in range(val)])
+        seen_now = lax.dynamic_update_slice_in_dim(
+            seen_now, s_next, (state_next ^ j0) * oldest, axis=1
+        )
+    return seen_now
 
 
 def passed_along(block, axis, distance):
@@ -84,7 +105,7 @@
     positions = jnp.where(token_at >= 0, seq_index * tok_count + token_at, -1)
     send_rows = picked.reshape(head_count, seq_count, per_owner, 3 * DH)
     send_places = positions.reshape(head_count, seq_count, per_owner)
-    rows_in = lax.all_to_all(send_rows, "seq", split_axis=1, concat_axis=1, tiled=True)
+    rows_in = order_sums_all(send_rows)
     places_in = lax.all_to_all(send_places, "seq", split_axis=1, concat_axis=1, tiled=True)
     item_count = rows_in.shape[0]
     owned = per_owner // most_rows

time: 283 us -> 269 us (0.951)
  waiting for transfers between devices: 114 us -> 86.9 us
  local copies, waits for them, and re-layouts: 79 us -> 87.9 us
  starting transfers between devices: 31.2 us -> 37.3 us
    all_to_all x1 -> x0, waiting for transfers between devices: 54.3 us -> none  [routed_part(): lax.all_to_all(send_rows, 'seq', split_axis=1, concat_axis=1, tiled=True)]
    all_to_all x1, waiting for transfers between devices: 0.01 us -> 19.8 us  [routed_part(): lax.all_to_all(send_places, 'seq', split_axis=1, concat_axis=1, tiled=True)]
    ppermute x0 -> x7, starting transfers between devices: none -> 9.68 us  [order_sums_all(): lax.ppermute(s_next, axis_tag, perm=[(num, num ^ j0) for num in range(val)])]
    ppermute x0 -> x7, waiting for transfers between devices: none -> 9.66 us  [order_sums_all(): lax.ppermute(s_next, axis_tag, perm=[(num, num ^ j0) for num in range(val)])]
    dynamic_update_slice x0 -> x7, local copies, waits for them, and re-layouts: none -> 5.43 us  [order_sums_all(): lax.dynamic_update_slice_in_dim(seen_now, s_next, (state_next ^ j0) * old...]
    all_to_all x1 -> x0, starting transfers between devices: 5.1 us -> none  [routed_part(): lax.all_to_all(send_rows, 'seq', split_axis=1, concat_axis=1, tiled=True)]
    all_to_all x1, starting transfers between devices: 16.2 us -> 19.3 us  [routed_part(): lax.all_to_all(result, 'seq', split_axis=1, concat_axis=1, tiled=True)]
    unnamed x25 -> x23, local copies, waits for them, and re-layouts: 13.7 us -> 15 us
  transfers between devices with their start and end apart: 5 -> 11, of which waited for: 3 -> 5; matrix products, arithmetic and copies ran while one was open for 29% -> 17% of each run, Pallas kernels for 0% -> 0%
where the time goes in v1:
time: 269 us; the launch traced here: 268 us
  local copies, waits for them, and re-layouts  87.9 us (33%)
  waiting for transfers between devices  86.9 us (32%)
  starting transfers between devices  37.3 us (14%)
  matrix products  32.1 us (12%)
  between operations  13.8 us (5%)
  other arithmetic  9.93 us (4%)
    reduce_scatter x1, waiting for transfers between devices, body(): lax.psum_scatter(group_sum.astype(jnp.bfloat16), 'heads', scatter_dimensi...  51.7 us
    gather x2, local copies, waits for them, and re-layouts, routed_part(): jnp.take_along_axis(row_data, jnp.maximum(token_at, 0)[:, :, None], axis=1)  44.7 us
    all_to_all x1, waiting for transfers between devices, routed_part(): lax.all_to_all(send_places, 'seq', split_axis=1, concat_axis=1, tiled=True)  19.8 us
    all_to_all x1, starting transfers between devices, routed_part(): lax.all_to_all(result, 'seq', split_axis=1, concat_axis=1, tiled=True)  19.3 us
    unnamed x23, local copies, waits for them, and re-layouts  15 us
    gather x2, local copies, waits for them, and re-layouts, routed_part(): mine = jnp.take_along_axis(returned, slot_index[:, :, None], axis=1)  11.3 us
    ppermute x7, starting transfers between devices, order_sums_all(): lax.ppermute(s_next, axis_tag, perm=[(num, num ^ j0) for num in range(val)])  9.68 us
    ppermute x7, waiting for transfers between devices, order_sums_all(): lax.ppermute(s_next, axis_tag, perm=[(num, num ^ j0) for num in range(val)])  9.66 us
  transfers between devices with their start and end apart: 11, of which 5 were waited for; matrix products, arithmetic and copies ran while one was open for 17% of the time, Pallas kernels for 0%

profile of v1, /device:TPU:0, one launch (start us, length us, event | category | flops | bytes accessed | tf_op | source)
XLA Modules:
  0.0 268.1 jit_solution(4236204611974657427)
XLA Ops:
  9.6 8.1 %scatter_custom_fusion = s32[4096]{0:T(1024)S(1)} fusion(s32[2048]{0:T(1024)S(1)} %bitcast.107, s32[2048]{0:T(1024)S(1)} %bitcast.108, s32[]{:T(128)} %constant.58.clone.1), kind=kCustom, calls=%fused_computation.62 | custom fusion | bytes 16388
  19.5 44.7 %gather_fusion = bf16[4096,384]{1,0:T(8,128)(2,1)} fusion(bf16[4,512,384]{2,1,0:T(8,128)(2,1)S(1)} %copy.81, s32[4096]{0:T(1024)S(1)} %bitcast.92), kind=kCustom, calls=%fused_computation | custom fusion | bytes 6324224 | tf_op jit(solution)/shard_map/jit(take_along_axis)/gather | solution.py:103
  64.2 3.4 %select_select_fusion = bf16[4,8,128,384]{3,2,1,0:T(8,128)(2,1)S(1)} fusion(bf16[4,8,128,384]{3,2,1,0:T(8,128)(2,1)} %bitcast.95, pred[4,8,128]{2,1,0:T(8,128)(4,1)S(1)} %get-tuple-element.36, pred[4,8,128]{2,1,0:T(8,128)(4,1)S(1)} %get-tuple-element.35), kind=kLoop, calls=%fused_computation.15 | loop fusion | flops 3145728 | bytes 6299648 | tf_op jit(solution)/shard_map/jit(_where)/select_n | solution.py:104
  68.1 1.6 constant_dynamic-slice_fusion
  70.1 2.6 collective-permute-start.2
  72.9 2.7 %collective-permute-start.4 = (bf16[4,1,128,384]{3,2,1,0:T(8,128)(2,1)}, bf16[4,1,128,384]{3,2,1,0:T(8,128)(2,1)}, u32[]{:S(2)}, u32[]{:S(2)}) collective-permute-start(bf16[4,1,128,384]{3,2,1,0:T(8,128)(2,1)} %get-tuple-element.24), channel_id=1, source_target_pairs={{0,4},{1,5},{2,6},{3,7},{4,0},{5,1},{6,2},{7,3},{8,12},{9,13},{10,... | collective-permute-start | bytes 1179656 | tf_op jit(solution)/shard_map/ppermute | solution.py:26
  76.2 4.9 %all-to-all-start = ((s32[4,8,128]{2,0,1:T(4,128)}), s32[4,8,128]{2,0,1:T(4,128)S(1)}, u32[]{:S(2)}, u32[]{:S(2)}) async-start(s32[4,8,128]{2,0,1:T(4,128)} %copy.73), calls=%async_computation | async-start | bytes 32768 | tf_op jit(solution)/shard_map/all_to_all | solution.py:109
  81.2 1.6 fusion.10
  82.8 2.3 slice.28
  85.1 1.9 slice.31
  86.9 2.3 copy.92
  89.2 2.0 copy.93
  91.3 19.8 %all-to-all-done = s32[4,8,128]{2,0,1:T(4,128)S(1)} async-done(((s32[4,8,128]{2,0,1:T(4,128)}), s32[4,8,128]{2,0,1:T(4,128)S(1)}, u32[]{:S(2)}, u32[]{:S(2)}) %all-to-all-start) | async-done | bytes 16416 | tf_op jit(solution)/shard_map/all_to_all | solution.py:109
  111.5 3.7 %collective-permute-start.6 = (bf16[4,1,128,384]{3,2,1,0:T(8,128)(2,1)}, bf16[4,1,128,384]{3,2,1,0:T(8,128)(2,1)S(1)}, u32[]{:S(2)}, u32[]{:S(2)}) collective-permute-start(bf16[4,1,128,384]{3,2,1,0:T(8,128)(2,1)} %get-tuple-element.16), channel_id=1, source_target_pairs={{0,6},{1,7},{2,4},{3,5},{4,2},{5,3},{6,0},{7,1},{8,14},{9,15},{10,... | collective-permute-start | bytes 1179656 | tf_op jit(solution)/shard_map/ppermute | solution.py:26
  116.4 1.1 constant_dynamic-update-slice_fusion.5
  117.5 3.2 %collective-permute-start = (bf16[2,512,512]{1,2,0:T(8,128)(2,1)}, bf16[2,512,512]{1,2,0:T(8,128)(2,1)}, u32[]{:S(2)}, u32[]{:S(2)}) collective-permute-start(bf16[2,512,512]{1,2,0:T(8,128)(2,1)} %copy.92), channel_id=1, source_target_pairs={{0,1},{1,2},{2,3},{3,4},{4,5},{5,6},{6,7},{8,9},{9,10},{10,11},{11... | collective-permute-start | bytes 3145736 | tf_op jit(solution)/shard_map/ppermute | solution.py:36
  121.7 1.1 constant_dynamic-update-slice_fusion.3
  123.8 1.8 collective-permute-done.6
  125.7 7.8 %collective-permute-done.7 = bf16[4,1,128,384]{3,2,1,0:T(8,128)(2,1)S(1)} collective-permute-done((bf16[4,1,128,384]{3,2,1,0:T(8,128)(2,1)}, bf16[4,1,128,384]{3,2,1,0:T(8,128)(2,1)S(1)}, u32[]{:S(2)}, u32[]{:S(2)}) %collective-permute-start.7) | collective-permute-done | bytes 393248 | tf_op jit(solution)/shard_map/ppermute | solution.py:26
  134.2 1.7 copy-done.2
  135.9 3.1 %multiply_select_fusion = f32[4,16,64,64]{2,3,1,0:T(8,128)S(1)} fusion(bf16[4,16,64,384]{3,2,1,0:T(8,128)(2,1)S(1)} %copy_bitcast_fusion, s32[4,16,64]{2,1,0:T(8,128)S(1)} %copy.77, pred[4,16,64]{2,1,0:T(8,128)(4,1)S(1)} %copy.76), kind=kOutput, calls=%fused_computation.20 | convolution fusion | flops 68157440 | bytes 3219456 | tf_op jit(solution)/shard_map/ncqd,nckd->ncqk/dot_general | solution.py:119
  139.5 2.0 fusion.11
  141.8 1.1 copy.85
  142.9 19.3 %all-to-all-start.1 = ((bf16[4,8,128,128]{3,2,0,1:T(8,128)(2,1)}), bf16[4,8,128,128]{3,2,0,1:T(8,128)(2,1)S(1)}, u32[]{:S(2)}, u32[]{:S(2)}) async-start(bf16[4,8,128,128]{3,2,0,1:T(8,128)(2,1)} %copy.85), calls=%async_computation.1 | async-start | bytes 2097152 | tf_op jit(solution)/shard_map/all_to_all | solution.py:136
  162.5 2.3 pad_maximum_fusion
  164.9 8.1 %fusion.33 = (f32[4,512]{1,0:T(4,128)S(1)}, f32[4,512,1024]{1,2,0:T(8,128)}) fusion(pred[512,1024]{0,1:T(8,128)(4,1)} %fusion.10, bf16[1024,4,128]{0,2,1:T(8,128)(2,1)} %bitcast.104, bf16[512,4,128]{0,2,1:T(8,128)(2,1)} %bitcast.106), kind=kOutput, calls=%fused_computation.88 | convolution fusion | flops 545260544 | bytes 10493952 | tf_op jit(solution)/shard_map/while/body/eval_jaxpr/sub | solution.py:42
  173.0 4.3 %fusion.12 = bf16[4,128,512]{2,1,0:T(8,128)(2,1)S(1)} fusion(bf16[1024,4,128]{0,2,1:T(8,128)(2,1)S(1)} %bitcast.103, f32[4,512,1024]{1,2,0:T(8,128)} %get-tuple-element.38, f32[4,512]{1,0:T(4,128)S(1)} %get-tuple-element.37), kind=kOutput, calls=%fused_computation.28 | convolution fusion | flops 541327360 | bytes 9969664 | tf_op jit(solution)/shard_map/while/body/eval_jaxpr/hqk,khd->qhd/dot_general | solution.py:68
  177.5 5.6 %fusion.35 = f32[512,4096]{1,0:T(8,128)} fusion(bf16[512,512]{0,1:T(8,128)(2,1)S(1)} %bitcast.105, bf16[512,4096]{1,0:T(8,128)(2,1)S(1)} %copy-done), kind=kOutput, calls=%fused_computation.90 | convolution fusion | flops 2147483648 | bytes 13107200 | tf_op jit(solution)/shard_map/dot_general | solution.py:145
  183.1 5.7 %all-to-all-done.1 = bf16[4,8,128,128]{3,2,0,1:T(8,128)(2,1)S(1)} async-done(((bf16[4,8,128,128]{3,2,0,1:T(8,128)(2,1)}), bf16[4,8,128,128]{3,2,0,1:T(8,128)(2,1)S(1)}, u32[]{:S(2)}, u32[]{:S(2)}) %all-to-all-start.1) | async-done | bytes 1048608 | tf_op jit(solution)/shard_map/all_to_all | solution.py:136
  189.0 11.1 %gather_fusion.1 = bf16[2048,128]{1,0:T(8,128)(2,1)S(1)} fusion(bf16[4,1024,128]{2,1,0:T(8,128)(2,1)S(1)} %bitcast.94, s32[2048]{0:T(1024)S(1)} %bitcast.93), kind=kCustom, calls=%fused_computation.1 | custom fusion | bytes 1064960 | tf_op jit(solution)/shard_map/jit(take_along_axis)/gather | solution.py:138
  200.4 9.0 %add_convert_fusion = bf16[512,4096]{1,0:T(8,128)(2,1)} fusion(f32[512,4096]{1,0:T(8,128)} %fusion.35, bf16[512,512]{0,1:T(8,128)(2,1)S(1)} %bitcast.99, bf16[512,4096]{1,0:T(8,128)(2,1)} %param.9), kind=kOutput, calls=%fused_computation.6 | convolution fusion | flops 2151677952 | bytes 17301504 | tf_op jit(solution)/shard_map/dot_general | solution.py:146
  209.5 51.7 %reduce-scatter.2.cloned.1.call-done = bf16[512,1024]{1,0:T(8,128)(2,1)} async-done(((bf16[512,4096]{1,0:T(8,128)(2,1)}), bf16[512,1024]{1,0:T(8,128)(2,1)}) %reduce-scatter.2.cloned.1.call-update) | async-done | bytes 1048592 | tf_op jit(solution)/shard_map/reduce_scatter | solution.py:147
  (74 shorter events, 12.5 us)
Async XLA Ops:
  6.5 2.2 copy-start.4
  7.5 2.0 copy-start.6
  7.5 2.0 copy-start.5
  8.4 9.4 %copy-start.3 = (bf16[3,512,512]{2,1,0:T(8,128)(2,1)S(1)}, bf16[3,512,512]{2,1,0:T(8,128)(2,1)}, u32[]{:S(2)}) copy-start(bf16[3,512,512]{2,1,0:T(8,128)(2,1)} %param.6) | copy-start | bytes 4718596
  69.7 41.9 %collective-permute-start.1 = (bf16[4,1,128,384]{3,2,1,0:T(8,128)(2,1)}, bf16[4,1,128,384]{3,2,1,0:T(8,128)(2,1)}, u32[]{:S(2)}, u32[]{:S(2)}) collective-permute-start(bf16[4,1,128,384]{3,2,1,0:T(8,128)(2,1)} %get-tuple-element.29), channel_id=1, source_target_pairs={{0,1},{1,0},{2,3},{3,2},{4,5},{5,4},{6,7},{7,6},{8,9},{9,8},{10,11... | collective-permute-start | bytes 1179656 | tf_op jit(solution)/shard_map/ppermute | solution.py:26
  70.1 46.2 %collective-permute-start.2 = (bf16[4,1,128,384]{3,2,1,0:T(8,128)(2,1)}, bf16[4,1,128,384]{3,2,1,0:T(8,128)(2,1)}, u32[]{:S(2)}, u32[]{:S(2)}) collective-permute-start(bf16[4,1,128,384]{3,2,1,0:T(8,128)(2,1)} %get-tuple-element.28), channel_id=1, source_target_pairs={{0,2},{1,3},{2,0},{3,1},{4,6},{5,7},{6,4},{7,5},{8,10},{9,11},{10,... | collective-permute-start | bytes 1179656 | tf_op jit(solution)/shard_map/ppermute | solution.py:26
  72.7 44.8 %collective-permute-start.3 = (bf16[4,1,128,384]{3,2,1,0:T(8,128)(2,1)}, bf16[4,1,128,384]{3,2,1,0:T(8,128)(2,1)}, u32[]{:S(2)}, u32[]{:S(2)}) collective-permute-start(bf16[4,1,128,384]{3,2,1,0:T(8,128)(2,1)} %get-tuple-element.26), channel_id=1, source_target_pairs={{0,3},{1,2},{2,1},{3,0},{4,7},{5,6},{6,5},{7,4},{8,11},{9,10},{10,... | collective-permute-start | bytes 1179656 | tf_op jit(solution)/shard_map/ppermute | solution.py:26
  72.9 48.8 %collective-permute-start.4 = (bf16[4,1,128,384]{3,2,1,0:T(8,128)(2,1)}, bf16[4,1,128,384]{3,2,1,0:T(8,128)(2,1)}, u32[]{:S(2)}, u32[]{:S(2)}) collective-permute-start(bf16[4,1,128,384]{3,2,1,0:T(8,128)(2,1)} %get-tuple-element.24), channel_id=1, source_target_pairs={{0,4},{1,5},{2,6},{3,7},{4,0},{5,1},{6,2},{7,3},{8,12},{9,13},{10,... | collective-permute-start | bytes 1179656 | tf_op jit(solution)/shard_map/ppermute | solution.py:26
  75.6 47.2 %collective-permute-start.5 = (bf16[4,1,128,384]{3,2,1,0:T(8,128)(2,1)}, bf16[4,1,128,384]{3,2,1,0:T(8,128)(2,1)}, u32[]{:S(2)}, u32[]{:S(2)}) collective-permute-start(bf16[4,1,128,384]{3,2,1,0:T(8,128)(2,1)} %get-tuple-element.17), channel_id=1, source_target_pairs={{0,5},{1,4},{2,7},{3,6},{4,1},{5,0},{6,3},{7,2},{8,13},{9,12},{10,... | collective-permute-start | bytes 1179656 | tf_op jit(solution)/shard_map/ppermute | solution.py:26
  76.2 34.8 %all-to-all-start = ((s32[4,8,128]{2,0,1:T(4,128)}), s32[4,8,128]{2,0,1:T(4,128)S(1)}, u32[]{:S(2)}, u32[]{:S(2)}) async-start(s32[4,8,128]{2,0,1:T(4,128)} %copy.73), calls=%async_computation | async-start | bytes 32768 | tf_op jit(solution)/shard_map/all_to_all | solution.py:109
  111.5 14.1 %collective-permute-start.6 = (bf16[4,1,128,384]{3,2,1,0:T(8,128)(2,1)}, bf16[4,1,128,384]{3,2,1,0:T(8,128)(2,1)S(1)}, u32[]{:S(2)}, u32[]{:S(2)}) collective-permute-start(bf16[4,1,128,384]{3,2,1,0:T(8,128)(2,1)} %get-tuple-element.16), channel_id=1, source_target_pairs={{0,6},{1,7},{2,4},{3,5},{4,2},{5,3},{6,0},{7,1},{8,14},{9,15},{10,... | collective-permute-start | bytes 1179656 | tf_op jit(solution)/shard_map/ppermute | solution.py:26
  116.3 17.2 %collective-permute-start.7 = (bf16[4,1,128,384]{3,2,1,0:T(8,128)(2,1)}, bf16[4,1,128,384]{3,2,1,0:T(8,128)(2,1)S(1)}, u32[]{:S(2)}, u32[]{:S(2)}) collective-permute-start(bf16[4,1,128,384]{3,2,1,0:T(8,128)(2,1)} %get-tuple-element.15), channel_id=1, source_target_pairs={{0,7},{1,6},{2,5},{3,4},{4,3},{5,2},{6,1},{7,0},{8,15},{9,14},{10,... | collective-permute-start | bytes 1179656 | tf_op jit(solution)/shard_map/ppermute | solution.py:26
  117.5 45.0 %collective-permute-start = (bf16[2,512,512]{1,2,0:T(8,128)(2,1)}, bf16[2,512,512]{1,2,0:T(8,128)(2,1)}, u32[]{:S(2)}, u32[]{:S(2)}) collective-permute-start(bf16[2,512,512]{1,2,0:T(8,128)(2,1)} %copy.92), channel_id=1, source_target_pairs={{0,1},{1,2},{2,3},{3,4},{4,5},{5,6},{6,7},{8,9},{9,10},{10,11},{11... | collective-permute-start | bytes 3145736 | tf_op jit(solution)/shard_map/ppermute | solution.py:36
  134.2 1.7 copy-start.2
  141.5 21.0 %copy-start.1 = (bf16[2,512,512]{1,2,0:T(8,128)(2,1)S(1)}, bf16[2,512,512]{1,2,0:T(8,128)(2,1)}, u32[]{:S(2)}) copy-start(bf16[2,512,512]{1,2,0:T(8,128)(2,1)} %copy.92) | copy-start | bytes 3145732
  142.9 45.9 %all-to-all-start.1 = ((bf16[4,8,128,128]{3,2,0,1:T(8,128)(2,1)}), bf16[4,8,128,128]{3,2,0,1:T(8,128)(2,1)S(1)}, u32[]{:S(2)}, u32[]{:S(2)}) async-start(bf16[4,8,128,128]{3,2,0,1:T(8,128)(2,1)} %copy.85), calls=%async_computation.1 | async-start | bytes 2097152 | tf_op jit(solution)/shard_map/all_to_all | solution.py:136
  162.3 98.9 %reduce-scatter.2.cloned.1.call-start = ((), (), s32[]{:S(2)}) async-start(), calls=%async_computation.3 | async-start | bytes 5242880 | tf_op jit(solution)/shard_map/reduce_scatter | solution.py:147
  173.0 4.6 %copy-start = (bf16[512,4096]{1,0:T(8,128)(2,1)S(1)}, bf16[512,4096]{1,0:T(8,128)(2,1)}, u32[]{:S(2)}) copy-start(bf16[512,4096]{1,0:T(8,128)(2,1)} %param.8) | copy-start | bytes 12582916
Sparse Core Ops, SparseCore 0:
  209.6 51.5 reduce-scatter.1
